TPU v7x, 32 devices: a whole 2x2x4 slice. The times are simulated.
32 devices in a mesh: blk: 8 (over y, x, core), grp: 4 (over z).
Axes of the slice: x: 2, y: 2, z: 4, core: 2. Of those that a mesh axis runs over, the one named last changes fastest.
Arguments:
- points: bfloat16 [16, 4096], P(None, ('blk', 'grp')), may hold values from -2 to 2, as said below
- right_side: float32 [64, 4096], P(None, ('blk', 'grp')), may hold values from -10 to 16
- nugget: float32 [4096], P(('blk', 'grp')), may hold values from 2 to 3
- scales: float32 [16], replicated, may hold values from 0.8 to 1.25
- pairs: int32 [8, 3], replicated, may hold values 0 or 1
Outputs:
- solution: float32 [64, 4096], P(None, ('blk', 'grp'))
- residual: float32 [64, 4096], P(None, ('blk', 'grp'))
Inputs may be any that keep to these rules, and one draw needn't show every extreme that they name: pairs[b, d - 1] is 1 when block b and block (b + d) mod 8 share a tile. In features 0 and 1 the points of block b lie on the circle of radius 8 / (2 pi) about the anchor, at arc lengths from b to b + 3 + 1 (measured round the circle from feature 1 = 0), one point in each of 512 equal slots of that arc; features 2 to 15 lie between 0 and 0.3.
All inputs are finite; a program needn't handle non-finite values.
Results may differ from a plain program's by a relative error of at most 0.0006.
Values may be sent and summed in bfloat16 or wider, within the bound.
No kernel may reach another device: no remote copies, remote signals or barrier semaphores. Data moves between devices by JAX's collectives and lax.ppermute only.
A program may use at most 64 MiB of HBM per device.

v0:
```python
import jax
import jax.numpy as jnp
from jax import lax
from jax.sharding import PartitionSpec as P

ITERS = 2


def passed_along(block, axis, distance):
    devices = range(lax.axis_size(axis))
    route = [((i - distance) % len(devices), i) for i in devices]
    return lax.ppermute(block, axis, route)


def kernel_tile(row_z, col_z):
    cross = jnp.dot(
        row_z.T, col_z, precision=lax.Precision.HIGHEST, preferred_element_type=jnp.float32
    )
    squared = (
        jnp.sum(row_z * row_z, axis=0)[:, None]
        + jnp.sum(col_z * col_z, axis=0)[None, :]
        - 2.0 * cross
    )
    distance = jnp.sqrt(jnp.maximum(squared, 0.0))
    spare = jnp.maximum(1.0 - distance, 0.0)
    return (spare**4 * (4.0 * distance + 1.0)).astype(jnp.bfloat16)


def tile_terms(row_z, column_block, scales):
    feat = row_z.shape[0]
    col_z = column_block[:feat].astype(jnp.float32) / scales[:, None]
    col_vec = column_block[feat:]
    total = col_z.shape[1]
    width = min(512, total)
    count = total // width
    nrhs = col_vec.shape[0]
    rows = row_z.shape[1]

    def step(carry, index):
        ahead, behind = carry
        start = index * width
        part_z = lax.dynamic_slice_in_dim(col_z, start, width, 1)
        part_v = lax.dynamic_slice_in_dim(col_vec, start, width, 1)
        tile = kernel_tile(row_z, part_z)
        ahead = ahead + lax.dot_general(
            part_v, tile, (((1,), (1,)), ((), ())), preferred_element_type=jnp.float32
        )
        return ((ahead, behind), None)

    start_carry = (jnp.zeros((nrhs, rows), jnp.float32), jnp.zeros((nrhs, total), jnp.float32))
    result, unused = lax.scan(step, start_carry, jnp.arange(count, dtype=jnp.int32))
    return result


def on_device(points, right_side, nugget, scales, pairs):
    nblk = lax.axis_size("blk")
    ngrp = lax.axis_size("grp")
    rows = points.shape[1]
    maxp = pairs.shape[1]
    nrhs = right_side.shape[0]
    total = rows * ngrp
    here = lax.axis_index("blk")
    amp = 1.0 / (total + 16)
    own_z = points.astype(jnp.float32) / scales[:, None]

    def squares(values):
        return lax.psum(jnp.sum(values * values, axis=1), ("blk", "grp"))

    solution = jnp.zeros(right_side.shape, jnp.float32)
    residual = right_side
    direction = right_side
    norm_now = squares(residual)
    for step in range(ITERS):
        rounded = direction.astype(jnp.bfloat16)
        stacked = jnp.concatenate([points, rounded], axis=0)
        own = lax.all_gather(stacked, "grp", axis=1, tiled=True)
        forward, unused = tile_terms(own_z, own, scales)
        for offset in range(1, maxp + 1):
            for sign in (1, -1):
                fetch_offset = sign * offset
                partner = passed_along(own, "blk", -fetch_offset)
                owner = here if sign == 1 else (here - offset) % nblk
                active = lax.dynamic_index_in_dim(pairs[:, offset - 1], owner, keepdims=False) == 1
                column_block = partner
                ahead, unused = lax.cond(
                    active,
                    lambda: tile_terms(own_z, column_block, scales),
                    lambda: (
                        jnp.zeros((nrhs, rows), jnp.float32),
                        jnp.zeros((nrhs, total), jnp.float32),
                    ),
                )
                forward = forward + ahead
        image = nugget[None, :] * direction + amp * forward
        alpha = norm_now / lax.psum(jnp.sum(direction * image, axis=1), ("blk", "grp"))
        solution = solution + alpha[:, None] * direction
        residual = residual - alpha[:, None] * image
        if step + 1 < ITERS:
            norm_next = squares(residual)
            direction = residual + (norm_next / norm_now)[:, None] * direction
            norm_now = norm_next
    return (solution, residual)


def solution(mesh):
    placed = (P(None, ("blk", "grp")), P(None, ("blk", "grp")), P(("blk", "grp")), P(), P())
    return jax.shard_map(
        on_device,
        mesh=mesh,
        in_specs=placed,
        out_specs=(P(None, ("blk", "grp")), P(None, ("blk", "grp"))),
        check_vma=False,
    )
```

profile of v0, /device:TPU:0, one launch (start us, length us, event | category | flops | bytes accessed | tf_op | source)
XLA Modules:
  0.0 181.6 jit_solution(10527828224152508425)
XLA Ops:
  0.6 0.8 convert_element_type.149
  1.4 13.8 %all_gather.6 = bf16[80,512]{1,0:T(8,128)(2,1)S(1)} all-gather(bf16[80,128]{1,0:T(8,128)(2,1)S(1)} %pad_maximum_fusion.1), channel_id=1, replica_groups=mesh['blk'=8,'grp'=4] {'grp'}, dimensions={1}, use_global_device_ids=true | all-gather | bytes 102400 | tf_op jit(solution)/shard_map/all_gather | solution.py:76
  15.2 1.7 collective-permute-start.4
  16.9 1.5 collective-permute-start.3
  18.4 1.4 collective-permute-start.2
  19.9 0.3 collective-permute-start.1
  20.3 0.6 multiply_convert_fusion.13
  21.0 0.2 fusion.92
  21.1 2.4 %collective-permute-start = (bf16[80,512]{1,0:T(8,128)(2,1)S(1)}, bf16[80,512]{1,0:T(8,128)(2,1)S(1)}, u32[]{:S(2)}, u32[]{:S(2)}) collective-permute-start(bf16[80,512]{1,0:T(8,128)(2,1)S(1)} %all_gather.6), channel_id=1, source_target_pairs={{4,0},{8,4},{12,8},{16,12},{20,16},{24,20},{28,24},{0,28},{5,1},{9... | collective-permute-start | bytes 245768 | tf_op jit(solution)/shard_map/ppermute | solution.py:12
  23.6 0.7 constant_dynamic-slice_fusion.1
  26.8 0.7 constant_dynamic-slice_fusion.5
  28.7 1.1 conditional.17
  28.9 0.8 multiply_convert_fusion.5
  29.6 0.2 convolution_bitcast_fusion.5
  29.8 1.1 conditional.16
  29.8 0.1 multiply_reduce_fusion.8
  29.9 0.8 multiply_convert_fusion.4
  30.7 0.2 convolution_bitcast_fusion.4
  31.0 1.1 conditional.13
  31.1 0.8 multiply_convert_fusion.1
  31.9 0.2 convolution_bitcast_fusion.1
  32.1 0.7 copy-done
  32.8 0.1 multiply_reduce_fusion.27
  32.9 41.9 %all-reduce = (f32[64]{0:T(128)S(1)}, f32[64]{0:T(128)S(1)}) all-reduce(f32[64]{0:T(128)S(1)} %get-tuple-element.357, f32[64]{0:T(128)S(1)} %get-tuple-element.356), channel_id=1, replica_groups=mesh['blk'=8,'grp'=4] {'blk','grp'}, use_global_device_ids=true, to_apply=%region_1.0 | all-reduce | flops 128 | bytes 1024 | tf_op jit(solution)/shard_map/psum | solution.py:67
  74.8 0.2 multiply_reduce_fusion.26
  75.0 40.3 %psum.30 = f32[64]{0:T(128)S(1)} all-reduce(f32[64]{0:T(128)S(1)} %multiply_reduce_fusion.26), channel_id=1, replica_groups=mesh['blk'=8,'grp'=4] {'blk','grp'}, use_global_device_ids=true, to_apply=%region_31.32 | all-reduce | flops 64 | bytes 512 | tf_op jit(solution)/shard_map/psum | solution.py:67
  115.5 12.1 %all_gather.7 = bf16[80,512]{1,0:T(8,128)(2,1)S(1)} all-gather(bf16[80,128]{1,0:T(8,128)(2,1)S(1)} %pad_maximum_fusion), channel_id=1, replica_groups=mesh['blk'=8,'grp'=4] {'grp'}, dimensions={1}, use_global_device_ids=true | all-gather | bytes 102400 | tf_op jit(solution)/shard_map/all_gather | solution.py:76
  127.6 1.7 collective-permute-start.10
  129.3 2.2 %collective-permute-start.9 = (bf16[80,512]{1,0:T(8,128)(2,1)S(1)}, bf16[80,512]{1,0:T(8,128)(2,1)S(1)}, u32[]{:S(2)}, u32[]{:S(2)}) collective-permute-start(bf16[80,512]{1,0:T(8,128)(2,1)S(1)} %all_gather.7), channel_id=1, source_target_pairs={{24,0},{28,4},{0,8},{4,12},{8,16},{12,20},{16,24},{20,28},{25,1},{... | collective-permute-start | bytes 245768 | tf_op jit(solution)/shard_map/ppermute | solution.py:12
  131.5 0.7 collective-permute-start.8
  132.4 0.6 multiply_convert_fusion.12
  133.0 2.7 %collective-permute-start.6 = (bf16[80,512]{1,0:T(8,128)(2,1)S(1)}, bf16[80,512]{1,0:T(8,128)(2,1)S(1)}, u32[]{:S(2)}, u32[]{:S(2)}) collective-permute-start(bf16[80,512]{1,0:T(8,128)(2,1)S(1)} %all_gather.7), channel_id=1, source_target_pairs={{4,0},{8,4},{12,8},{16,12},{20,16},{24,20},{28,24},{0,28},{5,1},{9... | collective-permute-start | bytes 245768 | tf_op jit(solution)/shard_map/ppermute | solution.py:12
  135.7 0.2 fusion.90
  135.9 1.1 conditional.23
  135.9 0.1 multiply_reduce_fusion.22
  136.0 0.8 multiply_convert_fusion.11
  136.8 0.2 convolution_bitcast_fusion.11
  136.9 1.1 conditional.22
  136.9 0.1 multiply_reduce_fusion.20
  137.0 0.8 multiply_convert_fusion.10
  137.8 0.2 convolution_bitcast_fusion.10
  138.1 0.3 collective-permute-done.7
  138.3 1.0 conditional.19
  138.4 0.8 multiply_convert_fusion.7
  139.2 0.2 convolution_bitcast_fusion.7
  139.4 0.1 multiply_reduce_fusion.24
  139.5 41.3 %psum.31 = f32[64]{0:T(128)S(1)} all-reduce(f32[64]{0:T(128)S(1)} %get-tuple-element.360), channel_id=1, replica_groups=mesh['blk'=8,'grp'=4] {'blk','grp'}, use_global_device_ids=true, to_apply=%region_58.59 | all-reduce | flops 64 | bytes 512 | tf_op jit(solution)/shard_map/psum | solution.py:95
  180.8 0.7 multiply_subtract_fusion
  (54 shorter events, 1.0 us)
Async XLA Ops:
  0.6 0.8 copy-start.2
  1.4 18.7 %copy-start.1 = (f32[16]{0:T(128)S(1)}, f32[16]{0:T(128)}, u32[]{:S(2)}) copy-start(f32[16]{0:T(128)} %param.32) | copy-start | bytes 196
  15.2 5.9 %collective-permute-start.5 = (bf16[80,512]{1,0:T(8,128)(2,1)S(1)}, bf16[80,512]{1,0:T(8,128)(2,1)S(1)}, u32[]{:S(2)}, u32[]{:S(2)}) collective-permute-start(bf16[80,512]{1,0:T(8,128)(2,1)S(1)} %all_gather.6), channel_id=1, source_target_pairs={{20,0},{24,4},{28,8},{0,12},{4,16},{8,20},{12,24},{16,28},{21,1},{... | collective-permute-start | bytes 245768 | tf_op jit(solution)/shard_map/ppermute | solution.py:12
  15.2 14.6 %collective-permute-start.4 = (bf16[80,512]{1,0:T(8,128)(2,1)S(1)}, bf16[80,512]{1,0:T(8,128)(2,1)S(1)}, u32[]{:S(2)}, u32[]{:S(2)}) collective-permute-start(bf16[80,512]{1,0:T(8,128)(2,1)S(1)} %all_gather.6), channel_id=1, source_target_pairs={{12,0},{16,4},{20,8},{24,12},{28,16},{0,20},{4,24},{8,28},{13,1},{... | collective-permute-start | bytes 245768 | tf_op jit(solution)/shard_map/ppermute | solution.py:12
  16.9 13.9 %collective-permute-start.3 = (bf16[80,512]{1,0:T(8,128)(2,1)S(1)}, bf16[80,512]{1,0:T(8,128)(2,1)S(1)}, u32[]{:S(2)}, u32[]{:S(2)}) collective-permute-start(bf16[80,512]{1,0:T(8,128)(2,1)S(1)} %all_gather.6), channel_id=1, source_target_pairs={{24,0},{28,4},{0,8},{4,12},{8,16},{12,20},{16,24},{20,28},{25,1},{... | collective-permute-start | bytes 245768 | tf_op jit(solution)/shard_map/ppermute | solution.py:12
  18.4 12.5 %collective-permute-start.2 = (bf16[80,512]{1,0:T(8,128)(2,1)S(1)}, bf16[80,512]{1,0:T(8,128)(2,1)S(1)}, u32[]{:S(2)}, u32[]{:S(2)}) collective-permute-start(bf16[80,512]{1,0:T(8,128)(2,1)S(1)} %all_gather.6), channel_id=1, source_target_pairs={{8,0},{12,4},{16,8},{20,12},{24,16},{28,20},{0,24},{4,28},{9,1},{1... | collective-permute-start | bytes 245768 | tf_op jit(solution)/shard_map/ppermute | solution.py:12
  19.9 11.1 %collective-permute-start.1 = (bf16[80,512]{1,0:T(8,128)(2,1)S(1)}, bf16[80,512]{1,0:T(8,128)(2,1)S(1)}, u32[]{:S(2)}, u32[]{:S(2)}) collective-permute-start(bf16[80,512]{1,0:T(8,128)(2,1)S(1)} %all_gather.6), channel_id=1, source_target_pairs={{28,0},{0,4},{4,8},{8,12},{12,16},{16,20},{20,24},{24,28},{29,1},{... | collective-permute-start | bytes 245768 | tf_op jit(solution)/shard_map/ppermute | solution.py:12
  21.0 2.6 %copy-start.4 = (s32[8,3]{0,1:T(4,128)S(1)}, s32[8,3]{0,1:T(4,128)}, u32[]{:S(2)}) copy-start(s32[8,3]{0,1:T(4,128)} %param.33) | copy-start | bytes 292
  21.1 10.9 %collective-permute-start = (bf16[80,512]{1,0:T(8,128)(2,1)S(1)}, bf16[80,512]{1,0:T(8,128)(2,1)S(1)}, u32[]{:S(2)}, u32[]{:S(2)}) collective-permute-start(bf16[80,512]{1,0:T(8,128)(2,1)S(1)} %all_gather.6), channel_id=1, source_target_pairs={{4,0},{8,4},{12,8},{16,12},{20,16},{24,20},{28,24},{0,28},{5,1},{9... | collective-permute-start | bytes 245768 | tf_op jit(solution)/shard_map/ppermute | solution.py:12
  32.0 0.8 copy-start
  32.1 0.7 copy-start.3
  127.6 5.4 %collective-permute-start.11 = (bf16[80,512]{1,0:T(8,128)(2,1)S(1)}, bf16[80,512]{1,0:T(8,128)(2,1)S(1)}, u32[]{:S(2)}, u32[]{:S(2)}) collective-permute-start(bf16[80,512]{1,0:T(8,128)(2,1)S(1)} %all_gather.7), channel_id=1, source_target_pairs={{20,0},{24,4},{28,8},{0,12},{4,16},{8,20},{12,24},{16,28},{21,1},{... | collective-permute-start | bytes 245768 | tf_op jit(solution)/shard_map/ppermute | solution.py:12
  127.6 9.3 %collective-permute-start.10 = (bf16[80,512]{1,0:T(8,128)(2,1)S(1)}, bf16[80,512]{1,0:T(8,128)(2,1)S(1)}, u32[]{:S(2)}, u32[]{:S(2)}) collective-permute-start(bf16[80,512]{1,0:T(8,128)(2,1)S(1)} %all_gather.7), channel_id=1, source_target_pairs={{12,0},{16,4},{20,8},{24,12},{28,16},{0,20},{4,24},{8,28},{13,1},{... | collective-permute-start | bytes 245768 | tf_op jit(solution)/shard_map/ppermute | solution.py:12
  129.3 8.6 %collective-permute-start.9 = (bf16[80,512]{1,0:T(8,128)(2,1)S(1)}, bf16[80,512]{1,0:T(8,128)(2,1)S(1)}, u32[]{:S(2)}, u32[]{:S(2)}) collective-permute-start(bf16[80,512]{1,0:T(8,128)(2,1)S(1)} %all_gather.7), channel_id=1, source_target_pairs={{24,0},{28,4},{0,8},{4,12},{8,16},{12,20},{16,24},{20,28},{25,1},{... | collective-permute-start | bytes 245768 | tf_op jit(solution)/shard_map/ppermute | solution.py:12
  131.5 6.5 %collective-permute-start.8 = (bf16[80,512]{1,0:T(8,128)(2,1)S(1)}, bf16[80,512]{1,0:T(8,128)(2,1)S(1)}, u32[]{:S(2)}, u32[]{:S(2)}) collective-permute-start(bf16[80,512]{1,0:T(8,128)(2,1)S(1)} %all_gather.7), channel_id=1, source_target_pairs={{8,0},{12,4},{16,8},{20,12},{24,16},{28,20},{0,24},{4,28},{9,1},{1... | collective-permute-start | bytes 245768 | tf_op jit(solution)/shard_map/ppermute | solution.py:12
  132.2 6.1 %collective-permute-start.7 = (bf16[80,512]{1,0:T(8,128)(2,1)S(1)}, bf16[80,512]{1,0:T(8,128)(2,1)S(1)}, u32[]{:S(2)}, u32[]{:S(2)}) collective-permute-start(bf16[80,512]{1,0:T(8,128)(2,1)S(1)} %all_gather.7), channel_id=1, source_target_pairs={{28,0},{0,4},{4,8},{8,12},{12,16},{16,20},{20,24},{24,28},{29,1},{... | collective-permute-start | bytes 245768 | tf_op jit(solution)/shard_map/ppermute | solution.py:12
  133.0 6.3 %collective-permute-start.6 = (bf16[80,512]{1,0:T(8,128)(2,1)S(1)}, bf16[80,512]{1,0:T(8,128)(2,1)S(1)}, u32[]{:S(2)}, u32[]{:S(2)}) collective-permute-start(bf16[80,512]{1,0:T(8,128)(2,1)S(1)} %all_gather.7), channel_id=1, source_target_pairs={{4,0},{8,4},{12,8},{16,12},{20,16},{24,20},{28,24},{0,28},{5,1},{9... | collective-permute-start | bytes 245768 | tf_op jit(solution)/shard_map/ppermute | solution.py:12
where the time goes:
time: 182 us
  blocking collectives  149 us (82%)
  starting transfers between devices  14.7 us (8%)
  matrix products  7.05 us (4%)
  between operations  4.71 us (3%)
  other arithmetic  2.96 us (2%)
  local copies, waits for them, and re-layouts  2.08 us (1%)
    psum x2, blocking collectives, squares(): return lax.psum(jnp.sum(values * values, axis=1), ('blk', 'grp'))  82.2 us
    psum x1, blocking collectives, on_device(): lax.psum(jnp.sum(direction * image, axis=1), ('blk', 'grp'))  41.3 us
    all_gather x2, blocking collectives, on_device(): own = lax.all_gather(stacked, 'grp', axis=1, tiled=True)  25.9 us
    ppermute x12, starting transfers between devices, passed_along(): return lax.ppermute(block, axis, route)  14.7 us
    dot_general x8, matrix products, kernel_tile(): jnp.dot(row_z.T, col_z, precision=lax.Precision.HIGHEST, preferred_elemen...  5.82 us
  transfers between devices with their start and end apart: 12, of which 1 were waited for; matrix products, arithmetic and copies ran while one was open for 5% of the time, Pallas kernels for 0%

commit v1 on v0

--- a/solution.py
+++ b/solution.py
@@ -73,7 +73,7 @@
     for step in range(ITERS):
         rounded = direction.astype(jnp.bfloat16)
         stacked = jnp.concatenate([points, rounded], axis=0)
-        own = lax.all_gather(stacked, "grp", axis=1, tiled=True)
+        own = jnp.concatenate(lax.all_gather(stacked, "grp"), axis=1)
         forward, unused = tile_terms(own_z, own, scales)
         for offset in range(1, maxp + 1):
             for sign in (1, -1):

time: 182 us -> 182 us (level)
  starting transfers between devices: 14.7 us -> 11.2 us
    ppermute x12, starting transfers between devices: 14.7 us -> 11.2 us  [passed_along(): return lax.ppermute(block, axis, route)]
    psum x1, blocking collectives: 41.3 us -> 38.8 us  [on_device(): lax.psum(jnp.sum(direction * image, axis=1), ('blk', 'grp'))]
    all_gather x2, blocking collectives: 25.9 us -> 28.2 us  [on_device(): own = jnp.concatenate(lax.all_gather(stacked, 'grp'), axis=1)]
    ppermute x12, waiting for transfers between devices: 0.31 us -> 2.13 us  [passed_along(): return lax.ppermute(block, axis, route)]
  transfers between devices with their start and end apart: 12 -> 12, of which waited for: 1 -> 2; matrix products, arithmetic and copies ran while one was open for 5% -> 4% of each run, Pallas kernels for 0% -> 0%
where the time goes in v1:
time: 182 us; the launch traced here: 181 us
  blocking collectives  150 us (82%)
  starting transfers between devices  11.2 us (6%)
  matrix products  7.04 us (4%)
  between operations  4.82 us (3%)
  other arithmetic  2.99 us (2%)
  waiting for transfers between devices  2.13 us (1%)
  local copies, waits for them, and re-layouts  2.09 us (1%)
    psum x2, blocking collectives, squares(): return lax.psum(jnp.sum(values * values, axis=1), ('blk', 'grp'))  83.5 us
    psum x1, blocking collectives, on_device(): lax.psum(jnp.sum(direction * image, axis=1), ('blk', 'grp'))  38.8 us
    all_gather x2, blocking collectives, on_device(): own = jnp.concatenate(lax.all_gather(stacked, 'grp'), axis=1)  28.2 us
    ppermute x12, starting transfers between devices, passed_along(): return lax.ppermute(block, axis, route)  11.2 us
    dot_general x8, matrix products, kernel_tile(): jnp.dot(row_z.T, col_z, precision=lax.Precision.HIGHEST, preferred_elemen...  5.82 us
  transfers between devices with their start and end apart: 12, of which 2 were waited for; matrix products, arithmetic and copies ran while one was open for 4% of the time, Pallas kernels for 0%

profile of v1, /device:TPU:0, one launch (start us, length us, event | category | flops | bytes accessed | tf_op | source)
XLA Modules:
  0.0 180.9 jit_solution(561359501911999106)
XLA Ops:
  0.6 0.8 convert_element_type.161
  1.4 14.9 %all-gather = bf16[320,128]{1,0:T(8,128)(2,1)S(1)} all-gather(bf16[80,128]{1,0:T(8,128)(2,1)S(1)} %pad_maximum_fusion.1), channel_id=2, replica_groups=mesh['blk'=8,'grp'=4] {'grp'}, dimensions={0}, use_global_device_ids=true | all-gather | bytes 102400 | tf_op jit(solution)/shard_map/all_gather | solution.py:76
  16.5 0.5 collective-permute-start.1
  17.0 2.4 %collective-permute-start.2 = (bf16[80,512]{1,0:T(8,128)(2,1)S(1)}, bf16[80,512]{1,0:T(8,128)(2,1)S(1)}, u32[]{:S(2)}, u32[]{:S(2)}) collective-permute-start(bf16[80,512]{1,0:T(8,128)(2,1)S(1)} %bitcast.224), channel_id=1, source_target_pairs={{8,0},{12,4},{16,8},{20,12},{24,16},{28,20},{0,24},{4,28},{9,1},{1... | collective-permute-start | bytes 245768 | tf_op jit(solution)/shard_map/ppermute | solution.py:12
  19.4 1.3 collective-permute-start.4
  20.8 0.1 fusion.98
  21.0 0.6 multiply_convert_fusion.13
  21.6 0.2 fusion.93
  21.8 0.9 collective-permute-start.5
  22.7 0.6 constant_dynamic-slice_fusion.5
  24.6 0.7 constant_dynamic-slice_fusion.1
  27.9 1.1 conditional.13
  28.0 0.8 multiply_convert_fusion.1
  28.8 0.2 convolution_bitcast_fusion.1
  29.1 1.1 conditional.16
  29.2 0.8 multiply_convert_fusion.4
  30.0 0.2 convolution_bitcast_fusion.4
  30.1 1.1 conditional.17
  30.3 0.8 multiply_convert_fusion.5
  31.0 0.2 convolution_bitcast_fusion.5
  31.2 0.6 copy-done.3
  31.9 0.1 multiply_reduce_fusion.26
  32.0 42.0 %all-reduce = (f32[64]{0:T(128)S(1)}, f32[64]{0:T(128)S(1)}) all-reduce(f32[64]{0:T(128)S(1)} %get-tuple-element.357, f32[64]{0:T(128)S(1)} %get-tuple-element.356), channel_id=1, replica_groups=mesh['blk'=8,'grp'=4] {'blk','grp'}, use_global_device_ids=true, to_apply=%region_1.0 | all-reduce | flops 128 | bytes 1024 | tf_op jit(solution)/shard_map/psum | solution.py:67
  74.0 0.2 multiply_reduce_fusion.25
  74.2 41.4 %psum.30 = f32[64]{0:T(128)S(1)} all-reduce(f32[64]{0:T(128)S(1)} %multiply_reduce_fusion.25), channel_id=1, replica_groups=mesh['blk'=8,'grp'=4] {'blk','grp'}, use_global_device_ids=true, to_apply=%region_31.32 | all-reduce | flops 64 | bytes 512 | tf_op jit(solution)/shard_map/psum | solution.py:67
  115.7 13.2 %all-gather.1 = bf16[320,128]{1,0:T(8,128)(2,1)S(1)} all-gather(bf16[80,128]{1,0:T(8,128)(2,1)S(1)} %pad_maximum_fusion), channel_id=3, replica_groups=mesh['blk'=8,'grp'=4] {'grp'}, dimensions={0}, use_global_device_ids=true | all-gather | bytes 102400 | tf_op jit(solution)/shard_map/all_gather | solution.py:76
  129.0 0.1 fusion.99
  129.2 0.5 collective-permute-start.7
  129.7 1.8 %collective-permute-start.8 = (bf16[80,512]{1,0:T(8,128)(2,1)S(1)}, bf16[80,512]{1,0:T(8,128)(2,1)S(1)}, u32[]{:S(2)}, u32[]{:S(2)}) collective-permute-start(bf16[80,512]{1,0:T(8,128)(2,1)S(1)} %bitcast.230), channel_id=1, source_target_pairs={{8,0},{12,4},{16,8},{20,12},{24,16},{28,20},{0,24},{4,28},{9,1},{1... | collective-permute-start | bytes 245768 | tf_op jit(solution)/shard_map/ppermute | solution.py:12
  131.5 0.4 collective-permute-start.9
  132.0 1.9 %collective-permute-start.10 = (bf16[80,512]{1,0:T(8,128)(2,1)S(1)}, bf16[80,512]{1,0:T(8,128)(2,1)S(1)}, u32[]{:S(2)}, u32[]{:S(2)}) collective-permute-start(bf16[80,512]{1,0:T(8,128)(2,1)S(1)} %bitcast.232), channel_id=1, source_target_pairs={{12,0},{16,4},{20,8},{24,12},{28,16},{0,20},{4,24},{8,28},{13,1},{... | collective-permute-start | bytes 245768 | tf_op jit(solution)/shard_map/ppermute | solution.py:12
  133.8 0.6 multiply_convert_fusion.12
  134.5 1.2 collective-permute-start.11
  135.8 0.2 fusion.90
  136.0 1.1 conditional.19
  136.1 0.8 multiply_convert_fusion.7
  136.9 0.2 convolution_bitcast_fusion.7
  137.1 1.3 collective-permute-done.9
  138.4 0.8 collective-permute-done.10
  139.2 1.0 conditional.22
  139.3 0.8 multiply_convert_fusion.10
  140.1 0.2 convolution_bitcast_fusion.10
  140.2 1.1 conditional.23
  140.4 0.8 multiply_convert_fusion.11
  141.1 0.2 convolution_bitcast_fusion.11
  141.3 0.1 multiply_reduce_fusion.24
  141.4 38.8 %psum.31 = f32[64]{0:T(128)S(1)} all-reduce(f32[64]{0:T(128)S(1)} %get-tuple-element.360), channel_id=1, replica_groups=mesh['blk'=8,'grp'=4] {'blk','grp'}, use_global_device_ids=true, to_apply=%region_58.59 | all-reduce | flops 64 | bytes 512 | tf_op jit(solution)/shard_map/psum | solution.py:95
  180.2 0.7 multiply_subtract_fusion
  (62 shorter events, 1.4 us)
Async XLA Ops:
  0.6 0.8 copy-start.2
  16.4 4.3 %copy-start.1 = (f32[16]{0:T(128)S(1)}, f32[16]{0:T(128)}, u32[]{:S(2)}) copy-start(f32[16]{0:T(128)} %param.32) | copy-start | bytes 196
  16.4 5.4 %collective-permute-start = (bf16[80,512]{1,0:T(8,128)(2,1)S(1)}, bf16[80,512]{1,0:T(8,128)(2,1)S(1)}, u32[]{:S(2)}, u32[]{:S(2)}) collective-permute-start(bf16[80,512]{1,0:T(8,128)(2,1)S(1)} %bitcast.222), channel_id=1, source_target_pairs={{4,0},{8,4},{12,8},{16,12},{20,16},{24,20},{28,24},{0,28},{5,1},{9... | collective-permute-start | bytes 245768 | tf_op jit(solution)/shard_map/ppermute | solution.py:12
  16.5 11.4 %collective-permute-start.1 = (bf16[80,512]{1,0:T(8,128)(2,1)S(1)}, bf16[80,512]{1,0:T(8,128)(2,1)S(1)}, u32[]{:S(2)}, u32[]{:S(2)}) collective-permute-start(bf16[80,512]{1,0:T(8,128)(2,1)S(1)} %bitcast.223), channel_id=1, source_target_pairs={{28,0},{0,4},{4,8},{8,12},{12,16},{16,20},{20,24},{24,28},{29,1},{... | collective-permute-start | bytes 245768 | tf_op jit(solution)/shard_map/ppermute | solution.py:12
  17.0 12.0 %collective-permute-start.2 = (bf16[80,512]{1,0:T(8,128)(2,1)S(1)}, bf16[80,512]{1,0:T(8,128)(2,1)S(1)}, u32[]{:S(2)}, u32[]{:S(2)}) collective-permute-start(bf16[80,512]{1,0:T(8,128)(2,1)S(1)} %bitcast.224), channel_id=1, source_target_pairs={{8,0},{12,4},{16,8},{20,12},{24,16},{28,20},{0,24},{4,28},{9,1},{1... | collective-permute-start | bytes 245768 | tf_op jit(solution)/shard_map/ppermute | solution.py:12
  19.4 9.6 %collective-permute-start.3 = (bf16[80,512]{1,0:T(8,128)(2,1)S(1)}, bf16[80,512]{1,0:T(8,128)(2,1)S(1)}, u32[]{:S(2)}, u32[]{:S(2)}) collective-permute-start(bf16[80,512]{1,0:T(8,128)(2,1)S(1)} %bitcast.225), channel_id=1, source_target_pairs={{24,0},{28,4},{0,8},{4,12},{8,16},{12,20},{16,24},{20,28},{25,1},{... | collective-permute-start | bytes 245768 | tf_op jit(solution)/shard_map/ppermute | solution.py:12
  19.4 9.6 %collective-permute-start.4 = (bf16[80,512]{1,0:T(8,128)(2,1)S(1)}, bf16[80,512]{1,0:T(8,128)(2,1)S(1)}, u32[]{:S(2)}, u32[]{:S(2)}) collective-permute-start(bf16[80,512]{1,0:T(8,128)(2,1)S(1)} %bitcast.226), channel_id=1, source_target_pairs={{12,0},{16,4},{20,8},{24,12},{28,16},{0,20},{4,24},{8,28},{13,1},{... | collective-permute-start | bytes 245768 | tf_op jit(solution)/shard_map/ppermute | solution.py:12
  21.6 1.1 copy-start.4
  21.8 8.3 %collective-permute-start.5 = (bf16[80,512]{1,0:T(8,128)(2,1)S(1)}, bf16[80,512]{1,0:T(8,128)(2,1)S(1)}, u32[]{:S(2)}, u32[]{:S(2)}) collective-permute-start(bf16[80,512]{1,0:T(8,128)(2,1)S(1)} %bitcast.227), channel_id=1, source_target_pairs={{20,0},{24,4},{28,8},{0,12},{4,16},{8,20},{12,24},{16,28},{21,1},{... | collective-permute-start | bytes 245768 | tf_op jit(solution)/shard_map/ppermute | solution.py:12
  30.1 1.1 copy-start
  31.2 0.7 copy-start.3
  129.1 5.4 %collective-permute-start.6 = (bf16[80,512]{1,0:T(8,128)(2,1)S(1)}, bf16[80,512]{1,0:T(8,128)(2,1)S(1)}, u32[]{:S(2)}, u32[]{:S(2)}) collective-permute-start(bf16[80,512]{1,0:T(8,128)(2,1)S(1)} %bitcast.228), channel_id=1, source_target_pairs={{4,0},{8,4},{12,8},{16,12},{20,16},{24,20},{28,24},{0,28},{5,1},{9... | collective-permute-start | bytes 245768 | tf_op jit(solution)/shard_map/ppermute | solution.py:12
  129.2 6.8 %collective-permute-start.7 = (bf16[80,512]{1,0:T(8,128)(2,1)S(1)}, bf16[80,512]{1,0:T(8,128)(2,1)S(1)}, u32[]{:S(2)}, u32[]{:S(2)}) collective-permute-start(bf16[80,512]{1,0:T(8,128)(2,1)S(1)} %bitcast.229), channel_id=1, source_target_pairs={{28,0},{0,4},{4,8},{8,12},{12,16},{16,20},{20,24},{24,28},{29,1},{... | collective-permute-start | bytes 245768 | tf_op jit(solution)/shard_map/ppermute | solution.py:12
  129.7 7.3 %collective-permute-start.8 = (bf16[80,512]{1,0:T(8,128)(2,1)S(1)}, bf16[80,512]{1,0:T(8,128)(2,1)S(1)}, u32[]{:S(2)}, u32[]{:S(2)}) collective-permute-start(bf16[80,512]{1,0:T(8,128)(2,1)S(1)} %bitcast.230), channel_id=1, source_target_pairs={{8,0},{12,4},{16,8},{20,12},{24,16},{28,20},{0,24},{4,28},{9,1},{1... | collective-permute-start | bytes 245768 | tf_op jit(solution)/shard_map/ppermute | solution.py:12
  131.5 6.9 %collective-permute-start.9 = (bf16[80,512]{1,0:T(8,128)(2,1)S(1)}, bf16[80,512]{1,0:T(8,128)(2,1)S(1)}, u32[]{:S(2)}, u32[]{:S(2)}) collective-permute-start(bf16[80,512]{1,0:T(8,128)(2,1)S(1)} %bitcast.231), channel_id=1, source_target_pairs={{24,0},{28,4},{0,8},{4,12},{8,16},{12,20},{16,24},{20,28},{25,1},{... | collective-permute-start | bytes 245768 | tf_op jit(solution)/shard_map/ppermute | solution.py:12
  132.0 7.2 %collective-permute-start.10 = (bf16[80,512]{1,0:T(8,128)(2,1)S(1)}, bf16[80,512]{1,0:T(8,128)(2,1)S(1)}, u32[]{:S(2)}, u32[]{:S(2)}) collective-permute-start(bf16[80,512]{1,0:T(8,128)(2,1)S(1)} %bitcast.232), channel_id=1, source_target_pairs={{12,0},{16,4},{20,8},{24,12},{28,16},{0,20},{4,24},{8,28},{13,1},{... | collective-permute-start | bytes 245768 | tf_op jit(solution)/shard_map/ppermute | solution.py:12
  134.5 5.7 %collective-permute-start.11 = (bf16[80,512]{1,0:T(8,128)(2,1)S(1)}, bf16[80,512]{1,0:T(8,128)(2,1)S(1)}, u32[]{:S(2)}, u32[]{:S(2)}) collective-permute-start(bf16[80,512]{1,0:T(8,128)(2,1)S(1)} %bitcast.233), channel_id=1, source_target_pairs={{20,0},{24,4},{28,8},{0,12},{4,16},{8,20},{12,24},{16,28},{21,1},{... | collective-permute-start | bytes 245768 | tf_op jit(solution)/shard_map/ppermute | solution.py:12
